TPU v7x, 512 devices: a whole 4x4x16 slice. The times are simulated.
512 devices in a mesh: ctx: 64 (over x, z), head: 8 (over y, core).
Axes of the slice: x: 4, y: 4, z: 16, core: 2. Of those that a mesh axis runs over, the one named last changes fastest.
Arguments:
- prefix_len: int32 [2], replicated, may hold values from 2048 to 16384, as said below
- page_slot: int32 [2, 64], replicated, may hold values from 0 to 127, as said below
- queries: bfloat16 [512, 8192], P('ctx', 'head'), may hold values from -6 to 6
- new_kv: bfloat16 [2, 512, 1024], P(None, 'ctx', 'head'), may hold values from -6 to 6
- cache: bfloat16 [2, 128, 256, 1024], P(None, 'ctx', None, 'head'), may hold values from -6 to 6
Outputs:
- attention: bfloat16 [512, 8192], P(('ctx', 'head'))
Inputs may be any that keep to these rules, and one draw needn't show every extreme that they name: `prefix_len`: each conversation's prefix holds 2048 to 16384 tokens; one conversation holds exactly 16384. `page_slot`: every slot number appears once; slot s lies at ctx index s // 2, as its slot s % 2.
All inputs are finite; a program needn't handle non-finite values.
Results may differ from a plain program's by a relative error of at most 0.0075.
Values may be sent and summed in bfloat16 or wider, within the bound.
A program may use at most 64 MiB of HBM per device.

v0:
```python
import jax
import jax.numpy as jnp
from jax import lax
from jax.sharding import PartitionSpec as P

HEAD_DIM = 128
SPAN = 256
PAGE = 256
MAXPAGES = 64
MASKED = -1e30


def slot_owners(page_slot, first_slot, slot_count):
    flat_table = page_slot.reshape(-1)
    wanted = first_slot + jnp.arange(slot_count, dtype=jnp.int32)
    matches = (flat_table[None, :] == wanted[:, None]).astype(jnp.int32)
    item_ids = jnp.arange(flat_table.shape[0], dtype=jnp.int32)
    return jnp.sum(matches * item_ids[None, :], axis=1)


def raise_rows(row_max, row_start, candidate):
    previous = lax.dynamic_slice_in_dim(row_max, row_start, candidate.shape[0], 0)
    return lax.dynamic_update_slice_in_dim(row_max, jnp.maximum(previous, candidate), row_start, 0)


def add_rows(totals, row_start, term):
    previous = lax.dynamic_slice_in_dim(totals, row_start, term.shape[0], 0)
    return lax.dynamic_update_slice_in_dim(totals, previous + term, row_start, 0)


def weigh_scores(scores, row_top):
    return jnp.exp(scores - row_top[..., None]).astype(jnp.bfloat16)


def local(prefix_len, page_slot, queries, new_kv, cache):
    own_rows = queries.shape[0]
    kv_local = new_kv.shape[2] // HEAD_DIM
    group_size = queries.shape[1] // HEAD_DIM // kv_local
    slot_count = cache.shape[1]
    score_scale = HEAD_DIM ** (-0.5)
    ctx_place = lax.axis_index("ctx")
    gathered = lax.all_gather(queries, "ctx", axis=0, tiled=True)
    total_rows = gathered.shape[0]
    gathered = gathered.reshape(total_rows, kv_local, group_size, HEAD_DIM)
    slot_items = slot_owners(page_slot, ctx_place * slot_count, slot_count)
    slot_dialog = slot_items // MAXPAGES
    slot_page = slot_items % MAXPAGES
    dialog_ids = jnp.arange(prefix_len.shape[0], dtype=jnp.int32)
    slot_length = jnp.sum(
        (dialog_ids[None, :] == slot_dialog[:, None]).astype(jnp.int32) * prefix_len[None, :],
        axis=1,
    )
    key_pages = cache[0].reshape(slot_count, PAGE, kv_local, HEAD_DIM)
    value_pages = cache[1].reshape(slot_count, PAGE, kv_local, HEAD_DIM)
    offsets = jnp.arange(PAGE, dtype=jnp.int32)

    def slot_start(slot_index):
        return slot_dialog[slot_index] * SPAN

    def slot_scores(slot_index):
        query_rows = lax.dynamic_slice_in_dim(gathered, slot_start(slot_index), SPAN, 0)
        page_keys = lax.dynamic_index_in_dim(key_pages, slot_index, 0, keepdims=False)
        raw_scores = (
            jnp.einsum("tghd,pgd->tghp", query_rows, page_keys, preferred_element_type=jnp.float32)
            * score_scale
        )
        live_keys = slot_page[slot_index] * PAGE + offsets < slot_length[slot_index]
        return jnp.where(live_keys, raw_scores, MASKED)

    def max_step(slot_index, row_max):
        return raise_rows(row_max, slot_start(slot_index), jnp.max(slot_scores(slot_index), axis=3))

    row_max = jnp.full((total_rows, kv_local, group_size), MASKED, jnp.float32)
    row_max = lax.fori_loop(0, slot_count, max_step, row_max)
    own_start = ctx_place * own_rows
    own_dialog_start = own_start // SPAN * SPAN
    own_offset = own_start % SPAN
    turn_steps = jnp.arange(SPAN, dtype=jnp.int32)
    own_steps = own_offset + jnp.arange(own_rows, dtype=jnp.int32)
    own_kv = new_kv.reshape(2, own_rows, kv_local, HEAD_DIM)
    dialog_queries = lax.dynamic_slice_in_dim(gathered, own_dialog_start, SPAN, 0)
    self_raw = (
        jnp.einsum("tghd,pgd->tghp", dialog_queries, own_kv[0], preferred_element_type=jnp.float32)
        * score_scale
    )
    causal = own_steps[None, :] <= turn_steps[:, None]
    self_scores = jnp.where(causal[:, None, None, :], self_raw, MASKED)
    self_values = own_kv[1]
    row_max = raise_rows(row_max, own_dialog_start, jnp.max(self_scores, axis=3))
    row_max = lax.pmax(row_max, "ctx")

    def slot_weights(slot_index):
        row_top = lax.dynamic_slice_in_dim(row_max, slot_start(slot_index), SPAN, 0)
        return weigh_scores(slot_scores(slot_index), row_top)

    def slot_values(slot_index, weights):
        page_values = lax.dynamic_index_in_dim(value_pages, slot_index, 0, keepdims=False)
        return jnp.einsum(
            "tghp,pgd->tghd", weights, page_values, preferred_element_type=jnp.float32
        )

    self_top = lax.dynamic_slice_in_dim(row_max, own_dialog_start, self_scores.shape[0], 0)
    self_weights = weigh_scores(self_scores, self_top)
    self_term = jnp.einsum(
        "tghp,pgd->tghd", self_weights, self_values, preferred_element_type=jnp.float32
    )
    self_sum = jnp.sum(self_weights.astype(jnp.float32), axis=3)
    weight_sums = jnp.zeros((total_rows, kv_local, group_size), jnp.float32)

    def sum_step(slot_index, carried):
        value_sums, weight_sums = carried
        row_start = slot_start(slot_index)
        weights = slot_weights(slot_index)
        return (
            add_rows(value_sums, row_start, slot_values(slot_index, weights)),
            add_rows(weight_sums, row_start, jnp.sum(weights.astype(jnp.float32), axis=3)),
        )

    value_sums = jnp.zeros((total_rows, kv_local, group_size, HEAD_DIM), jnp.float32)
    value_sums, weight_sums = lax.fori_loop(0, slot_count, sum_step, (value_sums, weight_sums))
    value_sums = add_rows(value_sums, own_dialog_start, self_term)
    own_sums = lax.psum_scatter(value_sums, "ctx", scatter_dimension=0, tiled=True)
    weight_sums = add_rows(weight_sums, own_dialog_start, self_sum)
    all_weights = lax.psum(weight_sums, "ctx")
    own_weights = lax.dynamic_slice_in_dim(all_weights, own_start, own_rows, 0)
    attention = (own_sums / own_weights[..., None]).astype(jnp.bfloat16)
    attention = attention.reshape(own_rows, kv_local * group_size * HEAD_DIM)
    return lax.all_to_all(attention, "head", split_axis=0, concat_axis=1, tiled=True)


def solution(mesh):
    return jax.shard_map(
        local,
        mesh=mesh,
        in_specs=(P(), P(), P("ctx", "head"), P(None, "ctx", "head"), P(None, "ctx", None, "head")),
        out_specs=P(("ctx", "head"), None),
        check_vma=False,
    )
```

profile of v0, /device:TPU:1, one launch (start us, length us, event | category | flops | bytes accessed | tf_op | source)
XLA Modules:
  0.0 1162.4 jit_solution(1225460248893137209)
XLA Ops:
  6.5 0.0 all-gather.2.cloned.1.call-start
  6.5 0.7 all-gather.2.cloned.1.call-update
  7.3 0.0 reduce-scatter.2.cloned.1.call-start
  7.3 0.8 eq.32
  8.1 1.0 slice_bitcast_fusion
  9.1 0.1 copy.51
  9.2 0.2 fusion.40
  9.4 0.8 fusion.41
  10.3 0.1 iota_compare_fusion
  10.3 134.7 %all-gather.2.cloned.1.call-done = bf16[512,1024]{1,0:T(8,128)(2,1)} async-done(((bf16[8,1024]{1,0:T(8,128)(2,1)}), bf16[512,1024]{1,0:T(8,128)(2,1)}) %all-gather.2.cloned.1.call-update) | async-done | bytes 1048592 | tf_op jit(solution)/shard_map/all_gather | solution.py:42
  145.1 1.5 copy.40
  146.6 0.7 copy.43
  147.2 0.0 copy-start.2
  147.3 8.8 while.30
  147.3 0.7 dynamic_slice.205
  148.6 0.6 dynamic_slice.207
  149.8 0.7 dynamic_slice.206
  150.5 0.7 fusion.55
  151.2 0.5 fusion.56
  151.6 0.7 dynamic_slice.205
  153.0 0.6 dynamic_slice.207
  154.2 0.7 dynamic_slice.206
  154.8 0.7 fusion.55
  155.5 0.5 fusion.56
  156.0 0.0 copy-done.2
  156.0 0.2 fusion.42
  156.3 222.5 %pmax.7 = f32[512,1,8]{0,2,1:T(8,128)S(1)} all-reduce(f32[512,1,8]{0,2,1:T(8,128)S(1)} %fusion.34), channel_id=1, replica_groups=mesh['ctx'=64,'head'=8] {'ctx'}, use_global_device_ids=true, to_apply=%region_6.7 | all-reduce | flops 4096 | bytes 32768 | tf_op jit(solution)/shard_map/pmax | solution.py:90
  378.8 0.2 broadcast_in_dim.64
  379.1 10.0 while.31
  379.1 0.7 dynamic_slice.214
  380.5 0.6 dynamic_slice.216
  381.6 0.7 dynamic_slice.215
  382.3 0.7 fusion.60
  383.0 0.7 convert_reduce_fusion.3
  383.6 0.4 fusion.61
  384.0 0.7 dynamic_slice.214
  385.4 0.6 dynamic_slice.216
  386.6 0.7 dynamic_slice.215
  387.2 0.7 fusion.60
  387.9 0.7 convert_reduce_fusion.3
  388.6 0.4 fusion.61
  389.0 1.8 copy.44
  390.8 1.9 copy.45
  392.7 0.0 copy-start
  392.7 1.7 fusion.28
  394.5 0.2 copy-done
  394.6 0.7 copy_dynamic-update-slice_fusion
  395.3 0.0 copy-start.1
  395.3 1.3 copy-done.1
  396.7 0.0 reduce-scatter.2.cloned.1.call-update
  396.7 0.1 copy.47
  396.9 0.1 copy.48
  397.0 218.9 %psum.7 = f32[512,1,8]{2,0,1:T(8,128)S(1)} all-reduce(f32[512,1,8]{2,0,1:T(8,128)S(1)} %constant_dynamic-update-slice_fusion), channel_id=1, replica_groups=mesh['ctx'=64,'head'=8] {'ctx'}, use_global_device_ids=true, to_apply=%region_12.13 | all-reduce | flops 4096 | bytes 32768 | tf_op jit(solution)/shard_map/psum | solution.py:124
  615.9 516.2 %reduce-scatter.2.cloned.1.call-done = f32[8,1,8,128]{3,2,1,0:T(8,128)} async-done(((f32[512,1,8,128]{3,2,1,0:T(8,128)}), f32[8,1,8,128]{3,2,1,0:T(8,128)}) %reduce-scatter.2.cloned.1.call-update) | async-done | bytes 32784 | tf_op jit(solution)/shard_map/reduce_scatter | solution.py:122
  1132.1 0.8 divide_convert_fusion
  1133.0 0.5 broadcast.127
  1133.5 0.7 reduce.9
  1134.3 20.6 %all_to_all.17 = bf16[8,2,512]{2,1,0:T(2,128)(2,1)S(1)} all-to-all(bf16[8,2,512]{2,1,0:T(2,128)(2,1)S(1)} %reshape.169), channel_id=1, replica_groups=mesh['ctx'=64,'head'=8] {'head'}, dimensions={0} | all-to-all | bytes 32768 | tf_op jit(solution)/shard_map/all_to_all | solution.py:128
  1154.9 0.6 reshape.170
  (19 shorter events, 0.2 us)
Async XLA Ops:
  6.5 138.5 %all-gather.2.cloned.1.call-start = ((), (), s32[]{:S(2)}) async-start(), calls=%async_computation.2 | async-start | bytes 1064960 | tf_op jit(solution)/shard_map/all_gather | solution.py:42
  7.3 1124.9 %reduce-scatter.2.cloned.1.call-start = ((), (), s32[]{:S(2)}) async-start(), calls=%async_computation.3 | async-start | bytes 2129920 | tf_op jit(solution)/shard_map/reduce_scatter | solution.py:122
  147.2 8.8 copy-start.2
  392.7 1.9 copy-start
  395.3 1.4 copy-start.1
Sparse Core Ops, SparseCore 0:
  10.3 134.7 all-gather.1
  396.8 735.2 reduce-scatter.1
where the time goes:
time: 1160 us
  waiting for transfers between devices  652 us (56%)
  blocking collectives  462 us (40%)
  local copies, waits for them, and re-layouts  19.3 us (2%)
  between operations  13.6 us (1%)
    reduce_scatter x1, waiting for transfers between devices, local(): lax.psum_scatter(value_sums, 'ctx', scatter_dimension=0, tiled=True)  516 us
    pmax x1, blocking collectives, local(): row_max = lax.pmax(row_max, 'ctx')  223 us
    psum x1, blocking collectives, local(): all_weights = lax.psum(weight_sums, 'ctx')  219 us
    all_gather x1, waiting for transfers between devices, local(): gathered = lax.all_gather(queries, 'ctx', axis=0, tiled=True)  135 us
  transfers between devices with their start and end apart: 2, of which 2 were waited for; matrix products, arithmetic and copies ran while one was open for 0% of the time, Pallas kernels for 0%

commit v1 on v0

--- a/solution.py
+++ b/solution.py
@@ -39,7 +39,9 @@
     slot_count = cache.shape[1]
     score_scale = HEAD_DIM ** (-0.5)
     ctx_place = lax.axis_index("ctx")
-    gathered = lax.all_gather(queries, "ctx", axis=0, tiled=True)
+    gathered = jnp.concatenate(
+        lax.all_to_all(jnp.stack([queries] * lax.axis_size("ctx")), "ctx", 0, 0), axis=0
+    )
     total_rows = gathered.shape[0]
     gathered = gathered.reshape(total_rows, kv_local, group_size, HEAD_DIM)
     slot_items = slot_owners(page_slot, ctx_place * slot_count, slot_count)

time: 1160 us -> 1090 us (0.940)
  waiting for transfers between devices: 652 us -> 558 us
  starting transfers between devices: 0.04 us -> 19.2 us
    all_gather x1 -> x0, waiting for transfers between devices: 135 us -> none  [local(): gathered = lax.all_gather(queries, 'ctx', axis=0, tiled=True)]
    all_to_all x0 -> x1, waiting for transfers between devices: none -> 49.5 us  [local(): lax.all_to_all(jnp.stack([queries] * lax.axis_size('ctx')), 'ctx', 0, 0)]
    all_to_all x0 -> x1, starting transfers between devices: none -> 19.1 us  [local(): lax.all_to_all(jnp.stack([queries] * lax.axis_size('ctx')), 'ctx', 0, 0)]
where the time goes in v1:
time: 1090 us
  waiting for transfers between devices  558 us (51%)
  blocking collectives  462 us (42%)
  starting transfers between devices  19.2 us (2%)
  local copies, waits for them, and re-layouts  17.8 us (2%)
  between operations  13.7 us (1%)
    reduce_scatter x1, waiting for transfers between devices, local(): lax.psum_scatter(value_sums, 'ctx', scatter_dimension=0, tiled=True)  509 us
    pmax x1, blocking collectives, local(): row_max = lax.pmax(row_max, 'ctx')  222 us
    psum x1, blocking collectives, local(): all_weights = lax.psum(weight_sums, 'ctx')  219 us
    all_to_all x1, waiting for transfers between devices, local(): lax.all_to_all(jnp.stack([queries] * lax.axis_size('ctx')), 'ctx', 0, 0)  49.5 us
  transfers between devices with their start and end apart: 2, of which 2 were waited for; matrix products, arithmetic and copies ran while one was open for 0% of the time, Pallas kernels for 0%

profile of v1, /device:TPU:1, one launch (start us, length us, event | category | flops | bytes accessed | tf_op | source)
XLA Modules:
  0.0 1086.1 jit_solution(3473644442290407952)
XLA Ops:
  6.5 0.0 copy-start.4
  6.5 0.0 copy-start.2
  6.5 0.0 copy-start.5
  6.5 1.9 stack.2
  8.4 19.1 %all-to-all-start = ((bf16[64,8,1024]{2,1,0:T(8,128)(2,1)}), bf16[64,8,1024]{2,1,0:T(8,128)(2,1)S(1)}, u32[]{:S(2)}, u32[]{:S(2)}) async-start(bf16[64,8,1024]{2,1,0:T(8,128)(2,1)} %stack.2), calls=%async_computation | async-start | bytes 2097152 | tf_op jit(solution)/shard_map/all_to_all | solution.py:43
  27.5 0.0 reduce-scatter.2.cloned.1.call-start
  27.6 0.0 copy-done.4
  27.6 0.1 eq.32
  27.7 0.0 copy-done.2
  27.7 0.1 copy.48
  27.9 0.2 fusion.39
  28.1 0.0 copy-done.5
  28.1 0.2 fusion.40
  28.3 0.1 iota_compare_fusion
  28.4 49.5 %all-to-all-done = bf16[64,8,1024]{2,1,0:T(8,128)(2,1)S(1)} async-done(((bf16[64,8,1024]{2,1,0:T(8,128)(2,1)}), bf16[64,8,1024]{2,1,0:T(8,128)(2,1)S(1)}, u32[]{:S(2)}, u32[]{:S(2)}) %all-to-all-start) | async-done | bytes 1048608 | tf_op jit(solution)/shard_map/all_to_all | solution.py:43
  77.9 0.3 copy.49
  78.1 0.1 copy.40
  78.3 0.0 copy-start.3
  78.3 8.7 while.30
  78.3 0.7 dynamic_slice.200
  79.7 0.7 dynamic_slice.201
  80.3 0.6 dynamic_slice.202
  81.5 0.7 fusion.54
  82.2 0.4 fusion.55
  82.7 0.7 dynamic_slice.200
  84.0 0.7 dynamic_slice.201
  84.7 0.6 dynamic_slice.202
  85.9 0.7 fusion.54
  86.6 0.5 fusion.55
  87.1 0.0 copy-done.3
  87.1 0.3 fusion.41
  87.4 222.3 %pmax.7 = f32[512,1,8]{0,2,1:T(8,128)S(1)} all-reduce(f32[512,1,8]{0,2,1:T(8,128)S(1)} %fusion.34), channel_id=1, replica_groups=mesh['ctx'=64,'head'=8] {'ctx'}, use_global_device_ids=true, to_apply=%region_6.7 | all-reduce | flops 4096 | bytes 32768 | tf_op jit(solution)/shard_map/pmax | solution.py:92
  309.7 0.2 broadcast_in_dim.64
  309.9 9.9 while.31
  309.9 0.7 dynamic_slice.209
  311.3 0.7 dynamic_slice.210
  312.0 0.6 dynamic_slice.211
  313.1 0.7 fusion.59
  313.8 0.7 convert_reduce_fusion.3
  314.5 0.4 fusion.60
  314.9 0.7 dynamic_slice.209
  316.3 0.7 dynamic_slice.210
  317.0 0.6 dynamic_slice.211
  318.1 0.7 fusion.59
  318.8 0.7 convert_reduce_fusion.3
  319.5 0.4 fusion.60
  319.9 1.9 copy.42
  321.8 1.8 copy.41
  323.6 0.0 copy-start
  323.6 1.7 fusion.28
  325.3 0.2 copy-done
  325.5 0.7 copy_dynamic-update-slice_fusion
  326.2 0.0 copy-start.1
  326.2 1.3 copy-done.1
  327.5 0.0 reduce-scatter.2.cloned.1.call-update
  327.6 0.1 copy.44
  327.7 0.1 copy.45
  327.9 219.0 %psum.7 = f32[512,1,8]{2,0,1:T(8,128)S(1)} all-reduce(f32[512,1,8]{2,0,1:T(8,128)S(1)} %constant_dynamic-update-slice_fusion), channel_id=1, replica_groups=mesh['ctx'=64,'head'=8] {'ctx'}, use_global_device_ids=true, to_apply=%region_12.13 | all-reduce | flops 4096 | bytes 32768 | tf_op jit(solution)/shard_map/psum | solution.py:126
  546.9 508.8 %reduce-scatter.2.cloned.1.call-done = f32[8,1,8,128]{3,2,1,0:T(8,128)} async-done(((f32[512,1,8,128]{3,2,1,0:T(8,128)}), f32[8,1,8,128]{3,2,1,0:T(8,128)}) %reduce-scatter.2.cloned.1.call-update) | async-done | bytes 32784 | tf_op jit(solution)/shard_map/reduce_scatter | solution.py:124
  1055.8 0.8 divide_convert_fusion
  1056.6 0.5 broadcast.129
  1057.2 0.7 reduce.9
  1057.9 20.7 %all_to_all.22 = bf16[8,2,512]{2,1,0:T(2,128)(2,1)S(1)} all-to-all(bf16[8,2,512]{2,1,0:T(2,128)(2,1)S(1)} %reshape.167), channel_id=1, replica_groups=mesh['ctx'=64,'head'=8] {'head'}, dimensions={0} | all-to-all | bytes 32768 | tf_op jit(solution)/shard_map/all_to_all | solution.py:130
  1078.6 0.6 reshape.168
  (21 shorter events, 0.3 us)
Async XLA Ops:
  6.5 21.1 %copy-start.4 = (s32[2,64]{1,0:T(2,128)S(1)}, s32[2,64]{1,0:T(2,128)}, u32[]{:S(2)}) copy-start(s32[2,64]{1,0:T(2,128)} %param.10) | copy-start | bytes 1540
  6.5 21.2 %copy-start.2 = (bf16[2,2,256,128]{3,2,1,0:T(8,128)(2,1)S(1)}, bf16[2,2,256,128]{3,2,1,0:T(8,128)(2,1)}, u32[]{:S(2)}) copy-start(bf16[2,2,256,128]{3,2,1,0:T(8,128)(2,1)} %param.13) | copy-start | bytes 786436
  6.5 21.6 %copy-start.5 = (s32[2]{0:T(128)S(1)}, s32[2]{0:T(128)}, u32[]{:S(2)}) copy-start(s32[2]{0:T(128)} %param.9) | copy-start | bytes 28
  8.4 69.4 %all-to-all-start = ((bf16[64,8,1024]{2,1,0:T(8,128)(2,1)}), bf16[64,8,1024]{2,1,0:T(8,128)(2,1)S(1)}, u32[]{:S(2)}, u32[]{:S(2)}) async-start(bf16[64,8,1024]{2,1,0:T(8,128)(2,1)} %stack.2), calls=%async_computation | async-start | bytes 2097152 | tf_op jit(solution)/shard_map/all_to_all | solution.py:43
  27.5 1028.2 %reduce-scatter.2.cloned.1.call-start = ((), (), s32[]{:S(2)}) async-start(), calls=%async_computation.3 | async-start | bytes 2129920 | tf_op jit(solution)/shard_map/reduce_scatter | solution.py:124
  78.3 8.8 copy-start.3
  323.6 1.9 copy-start
  326.2 1.4 copy-start.1
Sparse Core Ops, SparseCore 0:
  327.7 728.0 reduce-scatter.1
